TPU v7x, 128 devices: a whole 4x4x4 slice. The times are simulated.
128 devices in a mesh: dp: 4 (over y), row: 8 (over x, core), col: 4 (over z).
Axes of the slice: x: 4, y: 4, z: 4, core: 2. Of those that a mesh axis runs over, the one named last changes fastest.
Arguments:
- patches: bfloat16 [8, 128, 128, 768], P('dp', 'row', 'col'), may hold values from -64 to 64
- keep_mask: int32 [8, 128, 128], P('dp', 'row', 'col'), may hold values from 0 to 1, as said below
- mask_token: bfloat16 [768], replicated, may hold values from -6 to 6
- qkv_weight: bfloat16 [768, 2304], replicated, may hold values from -2 to 2
- out_weight: bfloat16 [768, 768], replicated, may hold values from -0.21875 to 0.21875
- up_weight: bfloat16 [768, 3072], P(None, 'dp'), may hold values from -0.21875 to 0.21875
- down_weight: bfloat16 [3072, 768], P('dp'), may hold values from -0.109375 to 0.109375
- dec_proj: bfloat16 [768, 256], replicated, may hold values from -0.21875 to 0.21875
- conv_weight: bfloat16 [2, 9, 256, 256], replicated, may hold values from -0.125 to 0.125
- head_weight: bfloat16 [256, 128], replicated, may hold values from -0.375 to 0.375
Outputs:
- recon: bfloat16 [8, 128, 128, 128], P('dp', 'row', 'col')
Inputs may be any that keep to these rules, and one draw needn't show every extreme that they name: `keep_mask`: each sample has exactly 4096 ones; in every sample the 16 x 32 tile of some device is all ones.
All inputs are finite; a program needn't handle non-finite values.
Results may differ from a plain program's by a relative error of at most 0.015.
Values may be sent and summed in bfloat16 or wider, within the bound.
No kernel may reach another device: no remote copies, remote signals or barrier semaphores. Data moves between devices by JAX's collectives and lax.ppermute only.
A program may use at most 192 MiB of HBM per device.

v0:
```python
import jax
import jax.numpy as jnp
from jax import lax
from jax.sharding import PartitionSpec as P

HEADS = 12
HD = 64
EPS = 1e-06
BLOCK = 512


def extended_2(cells, sides, width):
    for axis, dim in sides:
        count = lax.axis_size(axis)
        ends = count - 1
        head = lax.slice_in_dim(cells, 0, width, axis=dim)
        tail = lax.slice_in_dim(cells, cells.shape[dim] - width, cells.shape[dim], axis=dim)
        cells = jnp.concatenate(
            [
                lax.ppermute(tail, axis, [(i, (i + 1) % count) for i in range(ends)]),
                cells,
                lax.ppermute(head, axis, [((i + 1) % count, i) for i in range(ends)]),
            ],
            axis=dim,
        )
    return cells


def normalize(rows):
    wide = rows.astype(jnp.float32)
    mean = jnp.mean(wide, -1, keepdims=True)
    centred = wide - mean
    var = jnp.mean(centred * centred, -1, keepdims=True)
    return (centred * lax.rsqrt(var + EPS)).astype(jnp.bfloat16)


def attend(carry, query, keys, values):
    run_max, run_sum, store = carry
    scores = jnp.einsum("sqhd,skhd->shqk", query, keys, preferred_element_type=jnp.float32) * 0.125
    new_max = jnp.maximum(run_max, jnp.max(scores, -1))
    shrink = jnp.exp(run_max - new_max)
    expo = jnp.exp(scores - new_max[..., None])
    run_sum = run_sum * shrink + jnp.sum(expo, -1)
    added = jnp.einsum(
        "shqk,skhd->sqhd", expo.astype(jnp.bfloat16), values, preferred_element_type=jnp.float32
    )
    store = store * jnp.swapaxes(shrink, 1, 2)[..., None] + added
    return (new_max, run_sum, store)


def convolve(extended, taps, out_h, out_w):
    total = None
    for first in range(3):
        for second in range(3):
            term = jnp.einsum(
                "shwc,cd->shwd",
                extended[:, first : first + out_h, second : second + out_w],
                taps[first * 3 + second],
                preferred_element_type=jnp.float32,
            )
            total = term if total is None else total + term
    return total


def border(field):
    return extended_2(field, (("row", 1), ("col", 2)), 1)


def shards(
    patches,
    keep_mask,
    mask_token,
    qkv_weight,
    out_weight,
    up_weight,
    down_weight,
    dec_proj,
    conv_weight,
    head_weight,
):
    peers = lax.axis_size(("row", "col"))
    me = lax.axis_index(("row", "col"))
    samples, tile_h, tile_w, width = patches.shape
    tile = tile_h * tile_w
    cap = tile // peers
    kept_dev = tile // 4
    flat_tokens = patches.reshape(samples, tile, width)
    flat_mask = keep_mask.reshape(samples, tile)
    counts = jnp.sum(flat_mask, 1)
    every_count = lax.all_gather(counts[None, :], ("row", "col"), axis=0, tiled=True)
    ends = jnp.cumsum(every_count, 0)
    starts = ends - every_count
    my_start = lax.dynamic_index_in_dim(starts, me, 0, keepdims=False)
    running = jnp.cumsum(flat_mask, 1)
    positions = jnp.arange(tile, dtype=jnp.int32)
    kept_at = jnp.sum((running[:, None, :] <= positions[None, :, None]).astype(jnp.int32), 2)
    peer_ids = jnp.arange(peers, dtype=jnp.int32)
    slot_ids = jnp.arange(cap, dtype=jnp.int32)
    sample_ids = jnp.arange(samples, dtype=jnp.int32)[None, :, None]
    local_rank = slot_ids[None, None, :] * peers + jnp.mod(
        peer_ids[:, None, None] - my_start[None, :, None], peers
    )
    live = local_rank < counts[None, :, None]
    source_pos = kept_at[sample_ids, jnp.minimum(local_rank, tile - 1)]
    outgoing = jnp.where(
        live[..., None], flat_tokens[sample_ids, source_pos], jnp.zeros((), jnp.bfloat16)
    )
    arrived = lax.all_to_all(outgoing, ("row", "col"), split_axis=0, concat_axis=0, tiled=True)
    order_rank = jnp.arange(kept_dev, dtype=jnp.int32) * peers + me
    source_of = jnp.sum((ends[:, :, None] <= order_rank[None, None, :]).astype(jnp.int32), 0)
    start_of = jnp.take_along_axis(starts.T, source_of, 1)
    slot_of = (order_rank[None, :] - start_of) // peers
    rows_in = arrived[source_of, jnp.arange(samples, dtype=jnp.int32)[:, None], slot_of]
    flat_rows = rows_in.reshape(samples * kept_dev, width)
    normed = normalize(flat_rows)
    init_carry = (
        jnp.full((samples, HEADS, kept_dev), -1e30, jnp.float32),
        jnp.zeros((samples, HEADS, kept_dev), jnp.float32),
        jnp.zeros((samples, kept_dev, HEADS, HD), jnp.float32),
    )
    qkv = jnp.dot(normed, qkv_weight, preferred_element_type=jnp.float32).astype(jnp.bfloat16)
    query = qkv[:, :width].reshape(samples, kept_dev, HEADS, HD)
    keys_local = qkv[:, width : 2 * width].reshape(samples, kept_dev, width)
    values_local = qkv[:, 2 * width :].reshape(samples, kept_dev, width)
    carry = init_carry
    keys_piece = lax.all_gather(keys_local, ("row", "col"), axis=1, tiled=True)
    values_piece = lax.all_gather(values_local, ("row", "col"), axis=1, tiled=True)
    count = keys_piece.shape[1]
    for lower in range(0, count, BLOCK):
        upper = min(count, lower + BLOCK)
        keys_block = keys_piece[:, lower:upper].reshape(samples, upper - lower, HEADS, HD)
        values_block = values_piece[:, lower:upper].reshape(samples, upper - lower, HEADS, HD)
        carry = attend(carry, query, keys_block, values_block)
    run_max, run_sum, store = carry
    attn = (
        (store / jnp.swapaxes(run_sum, 1, 2)[..., None])
        .astype(jnp.bfloat16)
        .reshape(samples * kept_dev, width)
    )
    x_one = (
        flat_rows.astype(jnp.float32)
        + jnp.dot(attn, out_weight, preferred_element_type=jnp.float32)
    ).astype(jnp.bfloat16)
    normed_two = normalize(x_one)
    hidden = jax.nn.gelu(
        jnp.dot(
            normed_two,
            lax.all_gather(up_weight, "dp", axis=1, tiled=True),
            preferred_element_type=jnp.float32,
        ),
        approximate=False,
    ).astype(jnp.bfloat16)
    feed = jnp.dot(
        hidden,
        lax.all_gather(down_weight, "dp", axis=0, tiled=True),
        preferred_element_type=jnp.float32,
    )
    encoded = (
        (x_one.astype(jnp.float32) + feed).astype(jnp.bfloat16).reshape(samples, kept_dev, width)
    )
    back_rank = slot_ids[None, None, :] * peers + jnp.mod(me - starts[:, :, None], peers)
    back_live = back_rank < every_count[:, :, None]
    back_row = jnp.minimum((starts[:, :, None] + back_rank) // peers, kept_dev - 1)
    returning = jnp.where(
        back_live[..., None], encoded[sample_ids, back_row], jnp.zeros((), jnp.bfloat16)
    )
    home = lax.all_to_all(returning, ("row", "col"), split_axis=0, concat_axis=0, tiled=True)
    kept_rank = jnp.maximum(running - 1, 0)
    target_peer = jnp.mod(my_start[:, None] + kept_rank, peers)
    token_back = home[
        target_peer, jnp.arange(samples, dtype=jnp.int32)[:, None], kept_rank // peers
    ]
    filled = jnp.where(flat_mask[..., None] == 1, token_back, mask_token[None, None, :]).reshape(
        samples, tile_h, tile_w, width
    )
    h_zero = jnp.dot(filled, dec_proj, preferred_element_type=jnp.float32).astype(jnp.bfloat16)
    conv_one = convolve(border(h_zero), conv_weight[0], tile_h, tile_w)
    h_one = (h_zero.astype(jnp.float32) + jax.nn.gelu(conv_one, approximate=False)).astype(
        jnp.bfloat16
    )
    conv_two = convolve(border(h_one), conv_weight[1], tile_h, tile_w)
    h_two = (h_one.astype(jnp.float32) + jax.nn.gelu(conv_two, approximate=False)).astype(
        jnp.bfloat16
    )
    return jnp.dot(h_two, head_weight, preferred_element_type=jnp.float32).astype(jnp.bfloat16)


def solution(mesh):
    return jax.shard_map(
        shards,
        mesh=mesh,
        in_specs=(
            P("dp", "row", "col", None),
            P("dp", "row", "col"),
            P(),
            P(),
            P(),
            P(None, "dp"),
            P("dp", None),
            P(),
            P(),
            P(),
        ),
        out_specs=P("dp", "row", "col", None),
        check_vma=False,
    )
```

profile of v0, /device:TPU:2, one launch (start us, length us, event | category | flops | bytes accessed | tf_op | source)
XLA Modules:
  0.0 474.3 jit_solution(3876837634357682865)
XLA Ops:
  11.7 16.4 %all-reduce = s32[64]{0:T(128)} all-reduce(s32[64]{0:T(128)S(1)} %dynamic-update-slice), channel_id=2, replica_groups=mesh['dp'=4,'row'=8,'col'=4] {'row','col'}, use_global_device_ids=true, to_apply=%add | all-reduce | flops 64 | bytes 512
  41.8 9.1 %gather_fusion = s32[1024]{0:T(1024)S(1)} fusion(s32[2,512]{1,0:T(2,128)S(1)} %convert_reduce_fusion, s32[1024]{0:T(1024)S(1)} %reshape.722), kind=kCustom, calls=%fused_computation | custom fusion | bytes 16384 | tf_op jit(solution)/shard_map/gather | solution.py:104
  53.8 29.2 %gather_fusion.1 = bf16[1024,768]{1,0:T(8,128)(2,1)} fusion(bf16[2,512,768]{2,1,0:T(8,128)(2,1)} %bitcast.404, s32[1024]{0:T(1024)S(1)} %reshape.728), kind=kCustom, calls=%fused_computation.1 | custom fusion | bytes 3153920 | tf_op jit(solution)/shard_map/gather | solution.py:106
  85.9 6.6 %all-to-all-start = ((bf16[32,2,16,768]{3,2,1,0:T(8,128)(2,1)}), bf16[32,2,16,768]{3,2,1,0:T(8,128)(2,1)}, u32[]{:S(2)}, u32[]{:S(2)}) async-start(bf16[32,2,16,768]{3,2,1,0:T(8,128)(2,1)} %broadcast_select_fusion), calls=%async_computation | async-start | bytes 3145728 | tf_op jit(solution)/shard_map/all_to_all | solution.py:108
  99.3 14.7 %all-to-all-done = bf16[32,2,16,768]{3,2,1,0:T(8,128)(2,1)} async-done(((bf16[32,2,16,768]{3,2,1,0:T(8,128)(2,1)}), bf16[32,2,16,768]{3,2,1,0:T(8,128)(2,1)}, u32[]{:S(2)}, u32[]{:S(2)}) %all-to-all-start) | async-done | bytes 1572896 | tf_op jit(solution)/shard_map/all_to_all | solution.py:108
  114.0 4.2 gather_fusion.2
  126.2 61.5 %all-gather.6.cloned.1.call-done = bf16[2,4096,768]{2,1,0:T(8,128)(2,1)} async-done(((bf16[2,128,768]{2,1,0:T(8,128)(2,1)}), bf16[2,4096,768]{2,1,0:T(8,128)(2,1)}) %all-gather.6.cloned.1.call-update) | async-done | bytes 12582928 | tf_op jit(solution)/shard_map/all_gather | solution.py:126
  187.7 9.0 %fusion.404 = (bf16[2,512,768]{2,1,0:T(8,128)(2,1)}, bf16[2,512,768]{2,1,0:T(8,128)(2,1)S(1)}, bf16[2,512,768]{2,1,0:T(8,128)(2,1)}, bf16[2,512,768]{2,1,0:T(8,1...) fusion(bf16[2,4096,768]{2,1,0:T(8,128)(2,1)} %all-gather.6.clon, ...), kind=kLoop, calls=%fused_computation.479 | loop fusion | bytes 25165824 | tf_op jit(solution)/shard_map/slice | solution.py:131
  200.9 5.3 %multiply_reduce_fusion.7 = (f32[2,12,128]{2,1,0:T(8,128)S(1)}, f32[2,12,128,512]{3,2,1,0:T(8,128)}) fusion(bf16[2,512,12,64]{1,3,2,0:T(8,128)(2,1)} %bitcast.436, bf16[2,128,12,64]{1,0,3,2:T(2,128)(2,1)S(1)} %reshape.700), kind=kOutput, calls=%fused_computation.21 | convolution fusion | flops 204469248 | bytes 8269824 | tf_op jit(solution)/shard_map/sqhd,skhd->shqk/dot_general | solution.py:39
  211.6 3.7 multiply_reduce_fusion.1
  217.0 3.7 multiply_reduce_fusion.2
  242.3 6.8 %fusion.12 = (f32[2,12,128]{2,1,0:T(8,128)S(1)}, f32[2,12,128]{2,1,0:T(8,128)S(1)}) fusion(f32[2,12,128,512]{3,2,1,0:T(8,128)} %get-tuple-element.68, f32[2,12,128]{2,1,0:T(8,128)S(1)} %get-tuple-element.15, f32[2,12,128]{2,1,0:T(8,128)S(1)} %get-tuple-element.14, f32[2,12,128,512]{3,2,1,0:T(8,128)} %get-tuple-element.66), kind=kLoop, calls=%fused_computation.34 | loop fusion | flops 9431040 | bytes 12632064 | tf_op jit(solution)/shard_map/reduce_sum | solution.py:43
  249.3 4.7 fusion.8
  254.0 8.6 %fusion.403 = (bf16[2,512,768]{2,1,0:T(8,128)(2,1)}, bf16[2,512,768]{2,1,0:T(8,128)(2,1)}, bf16[2,512,768]{2,1,0:T(8,128)(2,1)S(1)}, bf16[2,512,768]{2,1,0:T(8,1...) fusion(bf16[2,4096,768]{2,1,0:T(8,128)(2,1)} %all-gather.8.clon, ...), kind=kLoop, calls=%fused_computation.478 | loop fusion | bytes 25165824 | tf_op jit(solution)/shard_map/slice | solution.py:132
  280.0 6.3 %fusion.4 = (f32[2,12,128]{2,1,0:T(8,128)S(1)}, f32[2,12,128]{2,1,0:T(8,128)S(1)}) fusion(f32[2,12,128,512]{3,2,1,0:T(8,128)} %get-tuple-element.76, f32[2,12,128]{2,1,0:T(8,128)S(1)} %get-tuple-element.19, f32[2,12,128]{2,1,0:T(8,128)S(1)} %get-tuple-element.18, f32[2,12,128,512]{3,2,1,0:T(8,128)} %get-tuple-element.74), kind=kLoop, calls=%fused_computation.26 | loop fusion | flops 9431040 | bytes 12632064 | tf_op jit(solution)/shard_map/reduce_sum | solution.py:43
  286.6 5.0 %fusion = (f32[2,12,128]{2,1,0:T(8,128)S(1)}, f32[2,12,128]{2,1,0:T(8,128)S(1)}) fusion(f32[2,12,128,512]{3,2,1,0:T(8,128)S(1)} %bitcast.416, f32[2,12,128]{2,1,0:T(8,128)S(1)} %get-tuple-element.56, f32[2,12,128]{2,1,0:T(8,128)S(1)} %get-tuple-element.20, f32[2,12,128,512]{3,2,1,0:T(8,128)} %get-tuple-element.78), kind=kLoop, calls=%fused_computation.22 | loop fusion | flops 9431040 | bytes 12632064 | tf_op jit(solution)/shard_map/reduce_sum | solution.py:43
  309.8 50.9 %all-gather.10.cloned.1.call-done = bf16[768,3072]{1,0:T(8,128)(2,1)} async-done(((bf16[768,768]{1,0:T(8,128)(2,1)}), bf16[768,3072]{1,0:T(8,128)(2,1)}) %all-gather.10.cloned.1.call-update) | async-done | bytes 4718608 | tf_op jit(solution)/shard_map/all_gather | solution.py:148
  360.7 12.7 %fusion.152 = bf16[256,768]{1,0:T(8,128)(2,1)S(1)} fusion(f32[256,768]{1,0:T(8,128)S(1)} %get-tuple-element.82, bf16[3072,768]{1,0:T(8,128)(2,1)} %all-gather.12.cloned.1.call-done, bf16[768,3072]{1,0:T(8,128)(2,1)} %all-gather.10.cloned.1.call-done, f32[256]{0:T(256)S(1)} %add_rsqrt_fusion, f32[256]{0:T(256)S(1)} %broadcast_multiply_fusion), kind=kOutput, calls=%fused_computation.136 | convolution fusion | flops 2468020224 | bytes 10618880 | tf_op jit(solution)/shard_map/dot_general | solution.py:153
  373.4 8.8 %gather_fusion.3 = bf16[1024,768]{1,0:T(8,128)(2,1)S(1)} fusion(bf16[2,128,768]{2,1,0:T(8,128)(2,1)S(1)} %bitcast.403, s32[1024]{0:T(1024)S(1)} %reshape.740), kind=kCustom, calls=%fused_computation.3 | custom fusion | bytes 3153920 | tf_op jit(solution)/shard_map/gather | solution.py:165
  383.7 7.6 %all-to-all-start.1 = ((bf16[32,2,16,768]{3,2,1,0:T(8,128)(2,1)}), bf16[32,2,16,768]{3,2,1,0:T(8,128)(2,1)S(1)}, u32[]{:S(2)}, u32[]{:S(2)}) async-start(bf16[32,2,16,768]{3,2,1,0:T(8,128)(2,1)} %broadcast_select_fusion.1), calls=%async_computation.1 | async-start | bytes 3145728 | tf_op jit(solution)/shard_map/all_to_all | solution.py:167
  391.4 21.3 %all-to-all-done.1 = bf16[32,2,16,768]{3,2,1,0:T(8,128)(2,1)S(1)} async-done(((bf16[32,2,16,768]{3,2,1,0:T(8,128)(2,1)}), bf16[32,2,16,768]{3,2,1,0:T(8,128)(2,1)S(1)}, u32[]{:S(2)}, u32[]{:S(2)}) %all-to-all-start.1) | async-done | bytes 1572896 | tf_op jit(solution)/shard_map/all_to_all | solution.py:167
  412.7 9.8 %gather_fusion.4 = bf16[1024,768]{1,0:T(8,128)(2,1)S(1)} fusion(bf16[32,2,16,768]{3,2,1,0:T(8,128)(2,1)S(1)} %all-to-all-done.1, s32[1024]{0:T(1024)S(1)} %bitcast.406), kind=kCustom, calls=%fused_computation.4 | custom fusion | bytes 3158016 | tf_op jit(solution)/shard_map/gather | solution.py:170
  436.0 3.9 collective-permute-done.3
  457.5 3.9 collective-permute-done.7
  (229 shorter events, 145.6 us)
Async XLA Ops:
  6.5 114.1 %copy-start = (bf16[768,2304]{1,0:T(8,128)(2,1)S(1)}, bf16[768,2304]{1,0:T(8,128)(2,1)}, u32[]{:S(2)}) copy-start(bf16[768,2304]{1,0:T(8,128)(2,1)} %param.13) | copy-start | bytes 10616836
  30.9 9.7 %copy-start.2 = (s32[32,2]{1,0:T(8,128)}, s32[32,2]{1,0:T(8,128)S(1)}, u32[]{:S(2)}) copy-start(s32[32,2]{1,0:T(8,128)S(1)} %get-tuple-element.6) | copy-start | bytes 772
  83.1 12.8 %copy-start.3 = (s32[32,2]{1,0:T(8,128)S(1)}, s32[32,2]{1,0:T(8,128)}, u32[]{:S(2)}) copy-start(s32[32,2]{1,0:T(8,128)} %copy-done.2) | copy-start | bytes 772
  85.9 28.1 %all-to-all-start = ((bf16[32,2,16,768]{3,2,1,0:T(8,128)(2,1)}), bf16[32,2,16,768]{3,2,1,0:T(8,128)(2,1)}, u32[]{:S(2)}, u32[]{:S(2)}) async-start(bf16[32,2,16,768]{3,2,1,0:T(8,128)(2,1)} %broadcast_select_fusion), calls=%async_computation | async-start | bytes 3145728 | tf_op jit(solution)/shard_map/all_to_all | solution.py:108
  92.5 95.2 %all-gather.6.cloned.1.call-start = ((), (), s32[]{:S(2)}) async-start(), calls=%async_computation.2 | async-start | bytes 12976128 | tf_op jit(solution)/shard_map/all_gather | solution.py:126
  123.7 130.3 %all-gather.8.cloned.1.call-start = ((), (), s32[]{:S(2)}) async-start(), calls=%async_computation.3 | async-start | bytes 12976128 | tf_op jit(solution)/shard_map/all_gather | solution.py:127
  124.5 185.3 %all-gather.12.cloned.1.call-start = ((), (), s32[]{:S(2)}) async-start(), calls=%async_computation.5 | async-start | bytes 5898240 | tf_op jit(solution)/shard_map/all_gather | solution.py:155
  125.2 235.5 %all-gather.10.cloned.1.call-start = ((), (), s32[]{:S(2)}) async-start(), calls=%async_computation.4 | async-start | bytes 5898240 | tf_op jit(solution)/shard_map/all_gather | solution.py:148
  280.0 13.6 %slice-start.14 = ((s8[6291456]{0:T(1024)(128)(4,1)}), s8[4194304]{0:T(1024)(128)(4,1)S(1)}, s32[]{:S(2)}) async-start(s8[6291456]{0:T(1024)(128)(4,1)} %bitcast.421), calls=%async_computation.20 | async-start | bytes 8388608
  286.6 8.9 %slice-start.12 = ((s8[6291456]{0:T(1024)(128)(4,1)}), s8[4194304]{0:T(1024)(128)(4,1)S(1)}, s32[]{:S(2)}) async-start(s8[6291456]{0:T(1024)(128)(4,1)} %bitcast.419), calls=%async_computation.18 | async-start | bytes 8388608
  373.4 8.8 %copy-start.17 = (pred[32,2,16]{2,1,0:T(4,128)(4,1)S(1)}, pred[32,2,16]{2,1,0:T(4,128)(4,1)}, u32[]{:S(2)}) copy-start(pred[32,2,16]{2,1,0:T(4,128)(4,1)} %get-tuple-element.61) | copy-start | bytes 3076
  382.2 9.0 %copy-start.18 = (s32[2,4,128]{2,1,0:T(4,128)S(1)}, s32[2,4,128]{2,1,0:T(4,128)}, u32[]{:S(2)}) copy-start(s32[2,4,128]{2,1,0:T(4,128)} %get-tuple-element.57) | copy-start | bytes 12292
  382.3 9.0 %copy-start.21 = (s32[2]{0:T(128)S(1)}, s32[2]{0:T(128)}, u32[]{:S(2)}) copy-start(s32[2]{0:T(128)} %copy-done.20) | copy-start | bytes 28
  382.3 9.1 %copy-start.15 = (s32[2,16,32]{2,1,0:T(8,128)S(1)}, s32[2,16,32]{2,1,0:T(8,128)}, u32[]{:S(2)}) copy-start(s32[2,16,32]{2,1,0:T(8,128)} %param.11) | copy-start | bytes 12292
  383.7 29.1 %all-to-all-start.1 = ((bf16[32,2,16,768]{3,2,1,0:T(8,128)(2,1)}), bf16[32,2,16,768]{3,2,1,0:T(8,128)(2,1)S(1)}, u32[]{:S(2)}, u32[]{:S(2)}) async-start(bf16[32,2,16,768]{3,2,1,0:T(8,128)(2,1)} %broadcast_select_fusion.1), calls=%async_computation.1 | async-start | bytes 3145728 | tf_op jit(solution)/shard_map/all_to_all | solution.py:167
  412.7 9.9 %copy-start.25 = (bf16[768]{0:T(1024)(128)(2,1)S(1)}, bf16[768]{0:T(1024)(128)(2,1)}, u32[]{:S(2)}) copy-start(bf16[768]{0:T(1024)(128)(2,1)} %param.12) | copy-start | bytes 4612
  424.4 4.7 collective-permute-start.1
  426.3 5.2 %collective-permute-start = (bf16[2,1,32,256]{3,2,1,0:T(8,128)(2,1)S(1)}, bf16[2,1,32,256]{3,2,1,0:T(8,128)(2,1)S(1)}, u32[]{:S(2)}, u32[]{:S(2)}) collective-permute-start(bf16[2,1,32,256]{3,2,1,0:T(8,128)(2,1)S(1)} %get-tuple-element.52), channel_id=1, source_target_pairs={{0,4},{4,8},{8,12},{12,16},{16,20},{20,24},{24,28},{1,5},{5,9},{9,... | collective-permute-start | bytes 98312 | tf_op jit(solution)/shard_map/ppermute | solution.py:20
  431.6 4.3 collective-permute-start.2
  434.0 5.9 %collective-permute-start.3 = (bf16[2,18,1,256]{3,2,1,0:T(2,128)(2,1)S(1)}, bf16[2,18,1,256]{3,2,1,0:T(2,128)(2,1)S(1)}, u32[]{:S(2)}, u32[]{:S(2)}) collective-permute-start(bf16[2,18,1,256]{3,2,1,0:T(2,128)(2,1)S(1)} %get-tuple-element.49), channel_id=1, source_target_pairs={{1,0},{2,1},{3,2},{5,4},{6,5},{7,6},{9,8},{10,9},{11,10},{13,12},{... | collective-permute-start | bytes 55304 | tf_op jit(solution)/shard_map/ppermute | solution.py:22
  445.0 4.6 collective-permute-start.5
  447.0 5.2 %collective-permute-start.4 = (bf16[2,1,32,256]{3,2,1,0:T(8,128)(2,1)S(1)}, bf16[2,1,32,256]{3,2,1,0:T(8,128)(2,1)S(1)}, u32[]{:S(2)}, u32[]{:S(2)}) collective-permute-start(bf16[2,1,32,256]{3,2,1,0:T(8,128)(2,1)S(1)} %get-tuple-element.50), channel_id=1, source_target_pairs={{0,4},{4,8},{8,12},{12,16},{16,20},{20,24},{24,28},{1,5},{5,9},{9,... | collective-permute-start | bytes 98312 | tf_op jit(solution)/shard_map/ppermute | solution.py:20
  452.3 5.2 %collective-permute-start.6 = (bf16[2,18,1,256]{3,2,1,0:T(2,128)(2,1)S(1)}, bf16[2,18,1,256]{3,2,1,0:T(2,128)(2,1)S(1)}, u32[]{:S(2)}, u32[]{:S(2)}) collective-permute-start(bf16[2,18,1,256]{3,2,1,0:T(2,128)(2,1)S(1)} %get-tuple-element.44), channel_id=1, source_target_pairs={{0,1},{1,2},{2,3},{4,5},{5,6},{6,7},{8,9},{9,10},{10,11},{12,13},{... | collective-permute-start | bytes 55304 | tf_op jit(solution)/shard_map/ppermute | solution.py:20
  455.6 5.9 %collective-permute-start.7 = (bf16[2,18,1,256]{3,2,1,0:T(2,128)(2,1)S(1)}, bf16[2,18,1,256]{3,2,1,0:T(2,128)(2,1)S(1)}, u32[]{:S(2)}, u32[]{:S(2)}) collective-permute-start(bf16[2,18,1,256]{3,2,1,0:T(2,128)(2,1)S(1)} %get-tuple-element.45), channel_id=1, source_target_pairs={{1,0},{2,1},{3,2},{5,4},{6,5},{7,6},{9,8},{10,9},{11,10},{13,12},{... | collective-permute-start | bytes 55304 | tf_op jit(solution)/shard_map/ppermute | solution.py:22
  (34 other events, 124.6 us)
Sparse Core Ops, SparseCore 0:
  123.9 63.7 all-gather.5
  190.0 62.3 all-gather.7
  254.1 52.0 all-gather.11
  307.7 52.9 all-gather.9
where the time goes:
time: 483 us; the launch traced here: 474 us
  waiting for transfers between devices  163 us (34%)
  local copies, waits for them, and re-layouts  128 us (27%)
  matrix products  72.7 us (15%)
  other arithmetic  48 us (10%)
  starting transfers between devices  31.4 us (7%)
  blocking collectives  16.4 us (3%)
  between operations  15 us (3%)
    all_gather x1, waiting for transfers between devices, shards(): keys_piece = lax.all_gather(keys_local, ('row', 'col'), axis=1, tiled=True)  61.5 us
    all_gather x1, waiting for transfers between devices, shards(): lax.all_gather(up_weight, 'dp', axis=1, tiled=True)  50.9 us
    dot_general x8, matrix products, attend(): jnp.einsum('sqhd,skhd->shqk', query, keys, preferred_element_type=jnp.flo...  30.9 us
    gather x1, local copies, waits for them, and re-layouts, shards(): flat_tokens[sample_ids, source_pos]  29.2 us
    slice x9, local copies, waits for them, and re-layouts, shards(): values_piece[:, lower:upper].reshape(samples, upper - lower, HEADS, HD)  25.9 us
    slice x9, local copies, waits for them, and re-layouts, shards(): keys_piece[:, lower:upper].reshape(samples, upper - lower, HEADS, HD)  23.6 us
    reduce_sum x4, other arithmetic, attend(): run_sum = run_sum * shrink + jnp.sum(expo, -1)  22.7 us
    all_to_all x1, waiting for transfers between devices, shards(): lax.all_to_all(returning, ('row', 'col'), split_axis=0, concat_axis=0, ti...  21.3 us
  transfers between devices with their start and end apart: 14, of which 8 were waited for; matrix products, arithmetic and copies ran while one was open for 27% of the time, Pallas kernels for 0%

commit v1 on v0

--- a/solution.py
+++ b/solution.py
@@ -123,7 +123,12 @@
     keys_local = qkv[:, width : 2 * width].reshape(samples, kept_dev, width)
     values_local = qkv[:, 2 * width :].reshape(samples, kept_dev, width)
     carry = init_carry
-    keys_piece = lax.all_gather(keys_local, ("row", "col"), axis=1, tiled=True)
+    keys_piece = jnp.concatenate(
+        lax.all_to_all(
+            jnp.stack([keys_local] * lax.axis_size(("row", "col"))), ("row", "col"), 0, 0
+        ),
+        axis=1,
+    )
     values_piece = lax.all_gather(values_local, ("row", "col"), axis=1, tiled=True)
     count = keys_piece.shape[1]
     for lower in range(0, count, BLOCK):

time: 483 us -> 603 us (1.25)
  the two profiles are of different devices: /device:TPU:2 before, /device:TPU:18 now
where the time goes in v1:
time: 603 us; the launch traced here: 592 us
  waiting for transfers between devices  232 us (38%)
  local copies, waits for them, and re-layouts  154 us (26%)
  matrix products  77.4 us (13%)
  starting transfers between devices  52.4 us (9%)
  other arithmetic  44.9 us (7%)
  blocking collectives  16.4 us (3%)
  between operations  15.1 us (3%)
    all_to_all x1, waiting for transfers between devices, shards(): lax.all_to_all(jnp.stack([keys_local] * lax.axis_size(('row', 'col'))), (...  182 us
    gather x1, local copies, waits for them, and re-layouts, shards(): flat_tokens[sample_ids, source_pos]  32.1 us
    dot_general x8, matrix products, attend(): jnp.einsum('sqhd,skhd->shqk', query, keys, preferred_element_type=jnp.flo...  28.5 us
    slice x9, local copies, waits for them, and re-layouts, shards(): values_piece[:, lower:upper].reshape(samples, upper - lower, HEADS, HD)  25.7 us
    slice x9, local copies, waits for them, and re-layouts, shards(): keys_piece[:, lower:upper].reshape(samples, upper - lower, HEADS, HD)  23.8 us
    all_to_all x1, starting transfers between devices, shards(): lax.all_to_all(returning, ('row', 'col'), split_axis=0, concat_axis=0, ti...  23.5 us
    dot_general x8, matrix products, attend(): jnp.einsum('shqk,skhd->sqhd', expo.astype(jnp.bfloat16), values, preferre...  22.2 us
    all_to_all x1, waiting for transfers between devices, shards(): lax.all_to_all(returning, ('row', 'col'), split_axis=0, concat_axis=0, ti...  21.3 us
  transfers between devices with their start and end apart: 14, of which 7 were waited for; matrix products, arithmetic and copies ran while one was open for 26% of the time, Pallas kernels for 0%

profile of v1, /device:TPU:18, one launch (start us, length us, event | category | flops | bytes accessed | tf_op | source)
XLA Modules:
  0.0 592.4 jit_solution(12743487238965291697)
XLA Ops:
  11.7 16.4 %all-reduce = s32[64]{0:T(128)} all-reduce(s32[64]{0:T(128)S(1)} %dynamic-update-slice), channel_id=2, replica_groups=mesh['dp'=4,'row'=8,'col'=4] {'row','col'}, use_global_device_ids=true, to_apply=%add | all-reduce | flops 64 | bytes 512
  41.7 9.1 %gather_fusion = s32[1024]{0:T(1024)S(1)} fusion(s32[2,512]{1,0:T(2,128)S(1)} %convert_reduce_fusion, s32[1024]{0:T(1024)S(1)} %reshape.728), kind=kCustom, calls=%fused_computation | custom fusion | bytes 16384 | tf_op jit(solution)/shard_map/gather | solution.py:104
  53.8 32.1 %gather_fusion.1 = bf16[1024,768]{1,0:T(8,128)(2,1)} fusion(bf16[2,512,768]{2,1,0:T(8,128)(2,1)} %bitcast.407, s32[1024]{0:T(1024)S(1)} %reshape.734), kind=kCustom, calls=%fused_computation.1 | custom fusion | bytes 3153920 | tf_op jit(solution)/shard_map/gather | solution.py:106
  88.7 5.4 all-to-all-start
  101.0 14.8 %all-to-all-done = bf16[32,2,16,768]{3,2,1,0:T(8,128)(2,1)} async-done(((bf16[32,2,16,768]{3,2,1,0:T(8,128)(2,1)}), bf16[32,2,16,768]{3,2,1,0:T(8,128)(2,1)}, u32[]{:S(2)}, u32[]{:S(2)}) %all-to-all-start) | async-done | bytes 1572896 | tf_op jit(solution)/shard_map/all_to_all | solution.py:108
  115.7 4.2 gather_fusion.2
  125.5 7.6 %stack.3 = bf16[32,2,128,768]{2,3,1,0:T(8,128)(2,1)} broadcast(bf16[2,128,768]{1,2,0:T(8,128)(2,1)S(1)} %copy.96), dimensions={1,2,3} | broadcast | bytes 12976128 | tf_op jit(solution)/shard_map/stack | solution.py:128
  133.1 6.2 %all-to-all-start.1 = ((bf16[32,2,128,768]{2,3,1,0:T(8,128)(2,1)}), bf16[32,2,128,768]{2,3,1,0:T(8,128)(2,1)}, u32[]{:S(2)}, u32[]{:S(2)}) async-start(bf16[32,2,128,768]{2,3,1,0:T(8,128)(2,1)} %stack.3), calls=%async_computation.1 | async-start | bytes 25165824 | tf_op jit(solution)/shard_map/all_to_all | solution.py:127
  141.2 181.9 %all-to-all-done.1 = bf16[32,2,128,768]{2,3,1,0:T(8,128)(2,1)} async-done(((bf16[32,2,128,768]{2,3,1,0:T(8,128)(2,1)}), bf16[32,2,128,768]{2,3,1,0:T(8,128)(2,1)}, u32[]{:S(2)}, u32[]{:S(2)}) %all-to-all-start.1) | async-done | bytes 12582944 | tf_op jit(solution)/shard_map/all_to_all | solution.py:127
  323.1 16.9 %copy.97 = bf16[32,2,128,768]{3,2,0,1:T(8,128)(2,1)} copy(bf16[32,2,128,768]{2,3,1,0:T(8,128)(2,1)} %all-to-all-done.1) | data formatting | bytes 25165824 | tf_op jit(solution)/shard_map/all_to_all | solution.py:127
  340.0 9.2 %fusion.404 = (bf16[2,512,768]{2,1,0:T(8,128)(2,1)}, bf16[2,512,768]{2,1,0:T(8,128)(2,1)S(1)}, bf16[2,512,768]{2,1,0:T(8,128)(2,1)}, bf16[2,512,768]{2,1,0:T(8,1...) fusion(bf16[2,4096,768]{2,1,0:T(8,128)(2,1)} %bitcast.426), kind=kLoop, calls=%fused_computation.479 | loop fusion | bytes 25165824 | tf_op jit(solution)/shard_map/slice | solution.py:136
  353.4 5.3 multiply_reduce_fusion.7
  392.4 8.9 %fusion.12 = (f32[2,12,128]{2,1,0:T(8,128)S(1)}, f32[2,12,128]{2,1,0:T(8,128)S(1)}) fusion(f32[2,12,128,512]{3,2,1,0:T(8,128)} %get-tuple-element.68, f32[2,12,128]{2,1,0:T(8,128)S(1)} %get-tuple-element.15, f32[2,12,128]{2,1,0:T(8,128)S(1)} %get-tuple-element.14, f32[2,12,128,512]{3,2,1,0:T(8,128)} %get-tuple-element.66), kind=kLoop, calls=%fused_computation.34 | loop fusion | flops 9431040 | bytes 12632064 | tf_op jit(solution)/shard_map/reduce_sum | solution.py:43
  401.6 4.9 fusion.8
  412.6 8.6 %fusion.403 = (bf16[2,512,768]{2,1,0:T(8,128)(2,1)}, bf16[2,512,768]{2,1,0:T(8,128)(2,1)}, bf16[2,512,768]{2,1,0:T(8,128)(2,1)S(1)}, bf16[2,512,768]{2,1,0:T(8,1...) fusion(bf16[2,4096,768]{2,1,0:T(8,128)(2,1)} %all-gather.5.clon, ...), kind=kLoop, calls=%fused_computation.478 | loop fusion | bytes 25165824 | tf_op jit(solution)/shard_map/slice | solution.py:137
  438.3 4.9 fusion.126
  447.1 3.9 fusion.132
  462.6 12.8 %fusion.152 = bf16[256,768]{1,0:T(8,128)(2,1)S(1)} fusion(f32[256,768]{1,0:T(8,128)S(1)} %get-tuple-element.82, bf16[3072,768]{1,0:T(8,128)(2,1)} %all-gather.9.cloned.1.call-done, bf16[768,3072]{1,0:T(8,128)(2,1)} %all-gather.7.cloned.1.call-done, f32[256]{0:T(256)S(1)} %add_rsqrt_fusion, f32[256]{0:T(256)S(1)} %broadcast_multiply_fusion), kind=kOutput, calls=%fused_computation.136 | convolution fusion | flops 2468020224 | bytes 10618880 | tf_op jit(solution)/shard_map/dot_general | solution.py:158
  475.4 9.0 %gather_fusion.3 = bf16[1024,768]{1,0:T(8,128)(2,1)S(1)} fusion(bf16[2,128,768]{2,1,0:T(8,128)(2,1)S(1)} %bitcast.406, s32[1024]{0:T(1024)S(1)} %reshape.746), kind=kCustom, calls=%fused_computation.3 | custom fusion | bytes 3153920 | tf_op jit(solution)/shard_map/gather | solution.py:170
  485.8 23.5 %all-to-all-start.2 = ((bf16[32,2,16,768]{3,2,1,0:T(8,128)(2,1)}), bf16[32,2,16,768]{3,2,1,0:T(8,128)(2,1)S(1)}, u32[]{:S(2)}, u32[]{:S(2)}) async-start(bf16[32,2,16,768]{3,2,1,0:T(8,128)(2,1)} %broadcast_select_fusion.1), calls=%async_computation.2 | async-start | bytes 3145728 | tf_op jit(solution)/shard_map/all_to_all | solution.py:172
  509.5 21.3 %all-to-all-done.2 = bf16[32,2,16,768]{3,2,1,0:T(8,128)(2,1)S(1)} async-done(((bf16[32,2,16,768]{3,2,1,0:T(8,128)(2,1)}), bf16[32,2,16,768]{3,2,1,0:T(8,128)(2,1)S(1)}, u32[]{:S(2)}, u32[]{:S(2)}) %all-to-all-start.2) | async-done | bytes 1572896 | tf_op jit(solution)/shard_map/all_to_all | solution.py:172
  530.8 9.8 %gather_fusion.4 = bf16[1024,768]{1,0:T(8,128)(2,1)S(1)} fusion(bf16[32,2,16,768]{3,2,1,0:T(8,128)(2,1)S(1)} %all-to-all-done.2, s32[1024]{0:T(1024)S(1)} %bitcast.409), kind=kCustom, calls=%fused_computation.4 | custom fusion | bytes 3158016 | tf_op jit(solution)/shard_map/gather | solution.py:175
  554.0 3.9 collective-permute-done.3
  575.6 3.9 collective-permute-done.7
  (231 shorter events, 152.9 us)
Async XLA Ops:
  6.5 115.8 %copy-start = (bf16[768,2304]{1,0:T(8,128)(2,1)S(1)}, bf16[768,2304]{1,0:T(8,128)(2,1)}, u32[]{:S(2)}) copy-start(bf16[768,2304]{1,0:T(8,128)(2,1)} %param.13) | copy-start | bytes 10616836
  85.9 11.6 %copy-start.3 = (s32[32,2]{1,0:T(8,128)S(1)}, s32[32,2]{1,0:T(8,128)}, u32[]{:S(2)}) copy-start(s32[32,2]{1,0:T(8,128)} %copy-done.2) | copy-start | bytes 772
  88.7 27.1 %all-to-all-start = ((bf16[32,2,16,768]{3,2,1,0:T(8,128)(2,1)}), bf16[32,2,16,768]{3,2,1,0:T(8,128)(2,1)}, u32[]{:S(2)}, u32[]{:S(2)}) async-start(bf16[32,2,16,768]{3,2,1,0:T(8,128)(2,1)} %broadcast_select_fusion), calls=%async_computation | async-start | bytes 3145728 | tf_op jit(solution)/shard_map/all_to_all | solution.py:108
  94.1 318.5 %all-gather.5.cloned.1.call-start = ((), (), s32[]{:S(2)}) async-start(), calls=%async_computation.3 | async-start | bytes 12976128 | tf_op jit(solution)/shard_map/all_gather | solution.py:132
  133.1 190.0 %all-to-all-start.1 = ((bf16[32,2,128,768]{2,3,1,0:T(8,128)(2,1)}), bf16[32,2,128,768]{2,3,1,0:T(8,128)(2,1)}, u32[]{:S(2)}, u32[]{:S(2)}) async-start(bf16[32,2,128,768]{2,3,1,0:T(8,128)(2,1)} %stack.3), calls=%async_computation.1 | async-start | bytes 25165824 | tf_op jit(solution)/shard_map/all_to_all | solution.py:127
  139.3 323.3 %all-gather.9.cloned.1.call-start = ((), (), s32[]{:S(2)}) async-start(), calls=%async_computation.5 | async-start | bytes 5898240 | tf_op jit(solution)/shard_map/all_gather | solution.py:160
  140.1 322.5 %all-gather.7.cloned.1.call-start = ((), (), s32[]{:S(2)}) async-start(), calls=%async_computation.4 | async-start | bytes 5898240 | tf_op jit(solution)/shard_map/all_gather | solution.py:153
  391.2 15.3 %slice-start.14 = ((s8[6291456]{0:T(1024)(128)(4,1)}), s8[4194304]{0:T(1024)(128)(4,1)S(1)}, s32[]{:S(2)}) async-start(s8[6291456]{0:T(1024)(128)(4,1)} %bitcast.424), calls=%async_computation.20 | async-start | bytes 8388608
  392.4 17.2 %copy-start.4 = (f32[2,12,128,512]{3,2,1,0:T(8,128)}, f32[2,12,128,512]{3,2,1,0:T(8,128)S(1)}, u32[]{:S(2)}) copy-start(f32[2,12,128,512]{3,2,1,0:T(8,128)S(1)} %get-tuple-element.78) | copy-start | bytes 18874372
  392.4 14.1 %slice-start.15 = ((s8[6291456]{0:T(1024)(128)(4,1)}), s8[2097152]{0:T(1024)(128)(4,1)S(1)}, s32[]{:S(2)}) async-start(s8[6291456]{0:T(1024)(128)(4,1)} %bitcast.424), calls=%async_computation.21 | async-start | bytes 4194304
  438.3 12.8 %slice-start.12 = ((s8[6291456]{0:T(1024)(128)(4,1)}), s8[4194304]{0:T(1024)(128)(4,1)S(1)}, s32[]{:S(2)}) async-start(s8[6291456]{0:T(1024)(128)(4,1)} %bitcast.422), calls=%async_computation.18 | async-start | bytes 8388608
  484.4 25.0 %copy-start.18 = (s32[2,4,128]{2,1,0:T(4,128)S(1)}, s32[2,4,128]{2,1,0:T(4,128)}, u32[]{:S(2)}) copy-start(s32[2,4,128]{2,1,0:T(4,128)} %get-tuple-element.57) | copy-start | bytes 12292
  484.4 25.0 %copy-start.21 = (s32[2]{0:T(128)S(1)}, s32[2]{0:T(128)}, u32[]{:S(2)}) copy-start(s32[2]{0:T(128)} %copy-done.20) | copy-start | bytes 28
  484.4 25.1 %copy-start.15 = (s32[2,16,32]{2,1,0:T(8,128)S(1)}, s32[2,16,32]{2,1,0:T(8,128)}, u32[]{:S(2)}) copy-start(s32[2,16,32]{2,1,0:T(8,128)} %param.11) | copy-start | bytes 12292
  485.8 45.0 %all-to-all-start.2 = ((bf16[32,2,16,768]{3,2,1,0:T(8,128)(2,1)}), bf16[32,2,16,768]{3,2,1,0:T(8,128)(2,1)S(1)}, u32[]{:S(2)}, u32[]{:S(2)}) async-start(bf16[32,2,16,768]{3,2,1,0:T(8,128)(2,1)} %broadcast_select_fusion.1), calls=%async_computation.2 | async-start | bytes 3145728 | tf_op jit(solution)/shard_map/all_to_all | solution.py:172
  530.8 9.9 %copy-start.25 = (bf16[768]{0:T(1024)(128)(2,1)S(1)}, bf16[768]{0:T(1024)(128)(2,1)}, u32[]{:S(2)}) copy-start(bf16[768]{0:T(1024)(128)(2,1)} %param.12) | copy-start | bytes 4612
  542.5 4.7 collective-permute-start.1
  544.4 5.2 collective-permute-start
  549.7 4.3 collective-permute-start.2
  552.1 5.9 collective-permute-start.3
  563.1 4.6 collective-permute-start.5
  565.1 5.2 collective-permute-start.4
  570.4 5.2 collective-permute-start.6
  573.7 5.9 collective-permute-start.7
  (34 other events, 151.2 us)
Sparse Core Ops, SparseCore 0:
  125.4 187.7 all-gather.4
  314.8 54.9 all-gather.8
  371.5 52.9 all-gather.6
